TPU v7x, 256 devices: a whole 4x4x8 slice. The times are simulated.
256 devices in a mesh: cell: 32 (over z, y_hi, core), period: 8 (over x, y_lo).
Axes of the slice: x: 4, y: 4 (y_hi: 2, y_lo: 2; y = y_hi * 2 + y_lo), z: 8, core: 2. Of those that a mesh axis runs over, the one named last changes fastest.
Arguments:
- footprints: float32 [32, 16, 32768], P(None, 'period', 'cell'), may hold values from -16 to 16
- cell_coords: int32 [2, 32768], P(None, 'cell'), may hold values from 0 to 255, as said below
- obs_period: int32 [32], replicated, may hold values from 0 to 15
- temporal_cov: float32 [16, 16], replicated, may hold values from -1.5 to 1.5
Outputs:
- hq_field: float32 [32, 16, 32768], P(None, 'period', 'cell')
- hqh_gram: float32 [32, 32], replicated
Inputs may be any that keep to these rules, and one draw needn't show every extreme that they name: `cell_coords`: cells sit at distinct grid points that together fill the rectangle of first coordinates 0 to 255 and second coordinates 0 to 127.
All inputs are finite; a program needn't handle non-finite values.
Results may differ from a plain program's by a relative error of at most 0.0003.
Values sent between devices are 32-bit elements; how exact they have to be, the bound alone decides.
No kernel may reach another device: no remote copies, remote signals or barrier semaphores. Data moves between devices by JAX's collectives and lax.ppermute only.
A program may use at most 64 MiB of HBM per device.

v0:
```python
import jax
import jax.numpy as jnp
from jax import lax
from jax.sharding import PartitionSpec as P

LENGTH_SCALE = 48.0
BLOCK_LIMIT = 4096


def covariance_tile(first_xy, second_xy):
    delta_x = first_xy[0][:, None] - second_xy[0][None, :]
    delta_y = first_xy[1][:, None] - second_xy[1][None, :]
    return jnp.exp(-jnp.sqrt(delta_x * delta_x + delta_y * delta_y) / LENGTH_SCALE)


def block_size(total_width, unit_width):
    unit_count = total_width // unit_width
    best_count = 1
    for factor in range(1, unit_count + 1):
        if unit_count % factor == 0 and factor * unit_width <= max(BLOCK_LIMIT, unit_width):
            best_count = factor
    return best_count * unit_width


def on_device(footprints, cell_coords, obs_period, temporal_cov):
    obs_count, per_local, cell_local = footprints.shape
    flat_count = obs_count * per_local
    period_first = lax.axis_index("period") * per_local
    period_ids = period_first + jnp.arange(per_local, dtype=jnp.int32)
    keep = (period_ids[None, :, None] <= obs_period[:, None, None]).astype(jnp.float32)
    masked = footprints * keep
    flat_rows = masked.reshape(flat_count, cell_local)
    local_places = cell_coords.astype(jnp.float32)
    empty = jnp.zeros((flat_count, cell_local), jnp.float32)
    piece_rows = lax.all_gather(flat_rows, "cell", axis=1, tiled=True)
    piece_places = lax.all_gather(local_places, "cell", axis=1, tiled=True)
    piece_width = piece_rows.shape[1]
    block_width = block_size(piece_width, cell_local)

    def add_block(block_index, running_sum):
        offset = block_index * block_width
        part_rows = lax.dynamic_slice_in_dim(piece_rows, offset, block_width, 1)
        part_places = lax.dynamic_slice_in_dim(piece_places, offset, block_width, 1)
        tile = covariance_tile(part_places, local_places)
        return running_sum + jnp.dot(
            part_rows, tile, precision=lax.Precision.HIGHEST, preferred_element_type=jnp.float32
        )

    spatial_flat = lax.fori_loop(0, piece_width // block_width, add_block, empty)
    spatial = spatial_flat.reshape(obs_count, per_local, cell_local)
    piece = lax.all_gather(spatial, "period", axis=1, tiled=True)
    weights = lax.dynamic_slice(temporal_cov, (period_first, 0), (per_local, piece.shape[1]))
    hq_field = jnp.einsum("tu,nuj->ntj", weights, piece, precision=lax.Precision.HIGHEST)
    partial_gram = jnp.einsum("ntj,mtj->nm", hq_field, masked, precision=lax.Precision.HIGHEST)
    hqh_gram = lax.psum(partial_gram, ("cell", "period"))
    return (hq_field, hqh_gram)


def solution(mesh):
    return jax.shard_map(
        on_device,
        mesh=mesh,
        in_specs=(P(None, "period", "cell"), P(None, "cell"), P(), P()),
        out_specs=(P(None, "period", "cell"), P()),
        check_vma=False,
    )
```

profile of v0, /device:TPU:1, one launch (start us, length us, event | category | flops | bytes accessed | tf_op | source)
XLA Modules:
  0.0 412.7 jit_solution(13719887616135554057)
XLA Ops:
  7.2 0.0 copy-start
  7.2 0.0 all-gather.3.cloned.1.call-start
  7.2 0.7 compare_convert_fusion
  8.0 0.1 copy.15
  8.1 1.1 broadcast_multiply_fusion
  9.2 0.9 reshape.51
  10.0 0.0 all-gather.3.cloned.1.call-update
  10.1 0.0 all-gather.5.cloned.1.call-start
  10.1 0.7 convert_element_type.12
  10.8 47.3 %all_gather.10 = f32[2,32768]{1,0:T(2,128)S(1)} all-gather(f32[2,1024]{1,0:T(2,128)S(1)} %convert_element_type.12), channel_id=1, replica_groups=mesh['cell'=32,'period'=8] {'cell'}, dimensions={1}, use_global_device_ids=true | all-gather | bytes 270336 | tf_op jit(solution)/shard_map/all_gather | solution.py:36
  58.1 58.6 %all-gather.3.cloned.1.call-done = f32[64,32768]{1,0:T(8,128)} async-done(((f32[64,1024]{1,0:T(8,128)}), f32[64,32768]{1,0:T(8,128)}) %all-gather.3.cloned.1.call-update) | async-done | bytes 8388624 | tf_op jit(solution)/shard_map/all_gather | solution.py:35
  116.7 157.3 %while.14 = (s32[]{:T(128)}, f32[64,1024]{1,0:T(8,128)S(1)}, f32[64,32768]{1,0:T(8,128)}, f32[2,32768]{1,0:T(2,128)S(1)}, f32[2,1024]{1,0:T(2,128)S(1)}, /*index...) while((s32[]{:T(128)}, f32[64,1024]{1,0:T(8,128)S(1)}, f32[64,32768]{1,0:T(8,128)}, ...), condition=%wide.region_1.0_spmd.clone, body=%wide.region_0.0_spmd.clone.sunk | while | flops 3250716672 | bytes 1695933 | solution.py:49
  116.7 0.1 constant_dynamic-slice_fusion.2
  116.8 19.5 %fusion.39 = f32[64,1024]{1,0:T(8,128)S(1)} fusion(f32[1024]{0:T(1024)S(1)} %bitcast.22, f32[4096]{0:T(1024)S(1)} %bitcast.20, f32[1024]{0:T(1024)S(1)} %bitcast.21, f32[4096]{0:T(1024)S(1)} %bitcast.19, f32[64,32768]{1,0:T(8,128)} %get-tuple-element.190, s32[]{:T(128)S(6)} %select_n.14, f32[64,1024]{1,0:T(8,128)S(1)} %get-tuple-element.179, ...), kind=kOutput, calls=%fused_computation.15.clone.1 | convolution fusion | flops 3250716672 | bytes 1613829 | tf_op jit(solution)/shard_map/while/body/eval_jaxpr/dot_general | solution.py:45
  136.3 0.1 constant_dynamic-slice_fusion.2
  136.4 19.5 %fusion.39 = f32[64,1024]{1,0:T(8,128)S(1)} fusion(f32[1024]{0:T(1024)S(1)} %bitcast.22, f32[4096]{0:T(1024)S(1)} %bitcast.20, f32[1024]{0:T(1024)S(1)} %bitcast.21, f32[4096]{0:T(1024)S(1)} %bitcast.19, f32[64,32768]{1,0:T(8,128)} %get-tuple-element.190, s32[]{:T(128)S(6)} %select_n.14, f32[64,1024]{1,0:T(8,128)S(1)} %get-tuple-element.179, ...), kind=kOutput, calls=%fused_computation.15.clone.1 | convolution fusion | flops 3250716672 | bytes 1613829 | tf_op jit(solution)/shard_map/while/body/eval_jaxpr/dot_general | solution.py:45
  156.0 0.1 constant_dynamic-slice_fusion.2
  156.1 19.5 %fusion.39 = f32[64,1024]{1,0:T(8,128)S(1)} fusion(f32[1024]{0:T(1024)S(1)} %bitcast.22, f32[4096]{0:T(1024)S(1)} %bitcast.20, f32[1024]{0:T(1024)S(1)} %bitcast.21, f32[4096]{0:T(1024)S(1)} %bitcast.19, f32[64,32768]{1,0:T(8,128)} %get-tuple-element.190, s32[]{:T(128)S(6)} %select_n.14, f32[64,1024]{1,0:T(8,128)S(1)} %get-tuple-element.179, ...), kind=kOutput, calls=%fused_computation.15.clone.1 | convolution fusion | flops 3250716672 | bytes 1613829 | tf_op jit(solution)/shard_map/while/body/eval_jaxpr/dot_general | solution.py:45
  175.6 0.1 constant_dynamic-slice_fusion.2
  175.7 19.5 %fusion.39 = f32[64,1024]{1,0:T(8,128)S(1)} fusion(f32[1024]{0:T(1024)S(1)} %bitcast.22, f32[4096]{0:T(1024)S(1)} %bitcast.20, f32[1024]{0:T(1024)S(1)} %bitcast.21, f32[4096]{0:T(1024)S(1)} %bitcast.19, f32[64,32768]{1,0:T(8,128)} %get-tuple-element.190, s32[]{:T(128)S(6)} %select_n.14, f32[64,1024]{1,0:T(8,128)S(1)} %get-tuple-element.179, ...), kind=kOutput, calls=%fused_computation.15.clone.1 | convolution fusion | flops 3250716672 | bytes 1613829 | tf_op jit(solution)/shard_map/while/body/eval_jaxpr/dot_general | solution.py:45
  195.3 0.1 constant_dynamic-slice_fusion.2
  195.4 19.5 %fusion.39 = f32[64,1024]{1,0:T(8,128)S(1)} fusion(f32[1024]{0:T(1024)S(1)} %bitcast.22, f32[4096]{0:T(1024)S(1)} %bitcast.20, f32[1024]{0:T(1024)S(1)} %bitcast.21, f32[4096]{0:T(1024)S(1)} %bitcast.19, f32[64,32768]{1,0:T(8,128)} %get-tuple-element.190, s32[]{:T(128)S(6)} %select_n.14, f32[64,1024]{1,0:T(8,128)S(1)} %get-tuple-element.179, ...), kind=kOutput, calls=%fused_computation.15.clone.1 | convolution fusion | flops 3250716672 | bytes 1613829 | tf_op jit(solution)/shard_map/while/body/eval_jaxpr/dot_general | solution.py:45
  214.9 0.1 constant_dynamic-slice_fusion.2
  215.0 19.5 %fusion.39 = f32[64,1024]{1,0:T(8,128)S(1)} fusion(f32[1024]{0:T(1024)S(1)} %bitcast.22, f32[4096]{0:T(1024)S(1)} %bitcast.20, f32[1024]{0:T(1024)S(1)} %bitcast.21, f32[4096]{0:T(1024)S(1)} %bitcast.19, f32[64,32768]{1,0:T(8,128)} %get-tuple-element.190, s32[]{:T(128)S(6)} %select_n.14, f32[64,1024]{1,0:T(8,128)S(1)} %get-tuple-element.179, ...), kind=kOutput, calls=%fused_computation.15.clone.1 | convolution fusion | flops 3250716672 | bytes 1613829 | tf_op jit(solution)/shard_map/while/body/eval_jaxpr/dot_general | solution.py:45
  234.6 0.1 constant_dynamic-slice_fusion.2
  234.7 19.5 %fusion.39 = f32[64,1024]{1,0:T(8,128)S(1)} fusion(f32[1024]{0:T(1024)S(1)} %bitcast.22, f32[4096]{0:T(1024)S(1)} %bitcast.20, f32[1024]{0:T(1024)S(1)} %bitcast.21, f32[4096]{0:T(1024)S(1)} %bitcast.19, f32[64,32768]{1,0:T(8,128)} %get-tuple-element.190, s32[]{:T(128)S(6)} %select_n.14, f32[64,1024]{1,0:T(8,128)S(1)} %get-tuple-element.179, ...), kind=kOutput, calls=%fused_computation.15.clone.1 | convolution fusion | flops 3250716672 | bytes 1613829 | tf_op jit(solution)/shard_map/while/body/eval_jaxpr/dot_general | solution.py:45
  254.2 0.1 constant_dynamic-slice_fusion.2
  254.3 19.5 %fusion.39 = f32[64,1024]{1,0:T(8,128)S(1)} fusion(f32[1024]{0:T(1024)S(1)} %bitcast.22, f32[4096]{0:T(1024)S(1)} %bitcast.20, f32[1024]{0:T(1024)S(1)} %bitcast.21, f32[4096]{0:T(1024)S(1)} %bitcast.19, f32[64,32768]{1,0:T(8,128)} %get-tuple-element.190, s32[]{:T(128)S(6)} %select_n.14, f32[64,1024]{1,0:T(8,128)S(1)} %get-tuple-element.179, ...), kind=kOutput, calls=%fused_computation.15.clone.1 | convolution fusion | flops 3250716672 | bytes 1613829 | tf_op jit(solution)/shard_map/while/body/eval_jaxpr/dot_general | solution.py:45
  274.0 0.1 reshape.52
  274.2 0.8 copy.16
  275.0 0.0 all-gather.5.cloned.1.call-update
  275.0 48.4 %all-gather.5.cloned.1.call-done = f32[32,16,1024]{2,0,1:T(8,128)} async-done(((f32[32,2,1024]{2,0,1:T(8,128)}), f32[32,16,1024]{2,0,1:T(8,128)}) %all-gather.5.cloned.1.call-update) | async-done | bytes 2097168 | tf_op jit(solution)/shard_map/all_gather | solution.py:51
  323.4 0.0 copy-done
  323.4 3.9 fusion.23
  327.3 0.0 copy-start.1
  327.3 0.5 convolution_bitcast_fusion
  327.7 78.1 %psum.7 = f32[32,32]{1,0:T(8,128)} all-reduce(f32[32,32]{1,0:T(8,128)S(1)} %convolution_bitcast_fusion), channel_id=1, replica_groups=mesh['cell'=32,'period'=8] {'cell','period'}, use_global_device_ids=true, to_apply=%region_2.0 | all-reduce | flops 1024 | bytes 8192 | tf_op jit(solution)/shard_map/psum | solution.py:55
  405.8 0.0 copy-done.1
  (10 shorter events, 0.1 us)
Async XLA Ops:
  7.2 316.2 %copy-start = (f32[16,16]{1,0:T(8,128)S(1)}, f32[16,16]{1,0:T(8,128)}, u32[]{:S(2)}) copy-start(f32[16,16]{1,0:T(8,128)} %param.9) | copy-start | bytes 3076
  7.2 109.5 %all-gather.3.cloned.1.call-start = ((), (), s32[]{:S(2)}) async-start(), calls=%async_computation | async-start | bytes 8650752 | tf_op jit(solution)/shard_map/all_gather | solution.py:35
  10.1 313.3 %all-gather.5.cloned.1.call-start = ((), (), s32[]{:S(2)}) async-start(), calls=%async_computation.1 | async-start | bytes 2359296 | tf_op jit(solution)/shard_map/all_gather | solution.py:51
  327.3 78.6 %copy-start.1 = (f32[32,2,1024]{2,1,0:T(2,128)}, f32[32,2,1024]{2,1,0:T(2,128)S(1)}, u32[]{:S(2)}) copy-start(f32[32,2,1024]{2,1,0:T(2,128)S(1)} %fusion.23) | copy-start | bytes 786436
Sparse Core Ops, SparseCore 0:
  11.4 105.2 all-gather.2
  275.1 48.2 all-gather.4
where the time goes:
time: 413 us
  matrix products  160 us (39%)
  blocking collectives  125 us (30%)
  waiting for transfers between devices  107 us (26%)
  between operations  14.1 us (3%)
    dot_general x8, matrix products, add_block(): jnp.dot(part_rows, tile, precision=lax.Precision.HIGHEST, preferred_eleme...  156 us
    psum x1, blocking collectives, on_device(): hqh_gram = lax.psum(partial_gram, ('cell', 'period'))  78.1 us
    all_gather x1, waiting for transfers between devices, on_device(): piece_rows = lax.all_gather(flat_rows, 'cell', axis=1, tiled=True)  58.6 us
    all_gather x1, waiting for transfers between devices, on_device(): piece = lax.all_gather(spatial, 'period', axis=1, tiled=True)  48.4 us
    all_gather x1, blocking collectives, on_device(): piece_places = lax.all_gather(local_places, 'cell', axis=1, tiled=True)  47.3 us
  transfers between devices with their start and end apart: 2, of which 2 were waited for; matrix products, arithmetic and copies ran while one was open for 0% of the time, Pallas kernels for 0%

commit v1 on v0

--- a/solution.py
+++ b/solution.py
@@ -5,6 +5,13 @@
 
 LENGTH_SCALE = 48.0
 BLOCK_LIMIT = 4096
+
+
+def swapped_in(x, mesh_axis, along):
+    size = lax.axis_size(mesh_axis)
+    blocks = jnp.stack([x for _ in range(size)])
+    blocks = lax.all_to_all(blocks, mesh_axis, split_axis=0, concat_axis=0)
+    return jnp.concatenate(blocks, axis=along)
 
 
 def covariance_tile(first_xy, second_xy):
@@ -48,7 +55,7 @@
 
     spatial_flat = lax.fori_loop(0, piece_width // block_width, add_block, empty)
     spatial = spatial_flat.reshape(obs_count, per_local, cell_local)
-    piece = lax.all_gather(spatial, "period", axis=1, tiled=True)
+    piece = swapped_in(spatial, "period", 1)
     weights = lax.dynamic_slice(temporal_cov, (period_first, 0), (per_local, piece.shape[1]))
     hq_field = jnp.einsum("tu,nuj->ntj", weights, piece, precision=lax.Precision.HIGHEST)
     partial_gram = jnp.einsum("ntj,mtj->nm", hq_field, masked, precision=lax.Precision.HIGHEST)

time: 413 us -> 399 us (0.966)
  waiting for transfers between devices: 107 us -> 89.8 us
  local copies, waits for them, and re-layouts: 2.84 us -> 9.42 us
    all_gather x1 -> x0, waiting for transfers between devices: 48.4 us -> none  [on_device(): piece = lax.all_gather(spatial, 'period', axis=1, tiled=True)]
    all_to_all x0 -> x1, waiting for transfers between devices: none -> 31 us  [swapped_in(): blocks = lax.all_to_all(blocks, mesh_axis, split_axis=0, concat_axis=0)]
    psum x1, blocking collectives: 78.1 us -> 73.5 us  [on_device(): hqh_gram = lax.psum(partial_gram, ('cell', 'period'))]
    reshape x2, local copies, waits for them, and re-layouts: 0.93 us -> 5.3 us  [swapped_in(): return jnp.concatenate(blocks, axis=along)]
where the time goes in v1:
time: 399 us
  matrix products  158 us (40%)
  blocking collectives  121 us (30%)
  waiting for transfers between devices  89.8 us (23%)
  between operations  14.1 us (4%)
  local copies, waits for them, and re-layouts  9.42 us (2%)
  starting transfers between devices  4.06 us (1%)
    dot_general x8, matrix products, add_block(): jnp.dot(part_rows, tile, precision=lax.Precision.HIGHEST, preferred_eleme...  156 us
    psum x1, blocking collectives, on_device(): hqh_gram = lax.psum(partial_gram, ('cell', 'period'))  73.5 us
    all_gather x1, waiting for transfers between devices, on_device(): piece_rows = lax.all_gather(flat_rows, 'cell', axis=1, tiled=True)  58.8 us
    all_gather x1, blocking collectives, on_device(): piece_places = lax.all_gather(local_places, 'cell', axis=1, tiled=True)  47.1 us
    all_to_all x1, waiting for transfers between devices, swapped_in(): blocks = lax.all_to_all(blocks, mesh_axis, split_axis=0, concat_axis=0)  31 us
  transfers between devices with their start and end apart: 2, of which 2 were waited for; matrix products, arithmetic and copies ran while one was open for 0% of the time, Pallas kernels for 0%

profile of v1, /device:TPU:1, one launch (start us, length us, event | category | flops | bytes accessed | tf_op | source)
XLA Modules:
  0.0 398.6 jit_solution(4095846216154310710)
XLA Ops:
  7.2 0.0 copy-start
  7.2 0.0 all-gather.2.cloned.1.call-start
  7.2 0.7 compare_convert_fusion
  8.0 0.1 copy.11
  8.1 1.1 broadcast_multiply_fusion
  9.2 0.9 reshape.56
  10.0 0.0 all-gather.2.cloned.1.call-update
  10.1 0.7 convert_element_type.12
  10.8 47.1 %all_gather.7 = f32[2,32768]{1,0:T(2,128)S(1)} all-gather(f32[2,1024]{1,0:T(2,128)S(1)} %convert_element_type.12), channel_id=1, replica_groups=mesh['cell'=32,'period'=8] {'cell'}, dimensions={1}, use_global_device_ids=true | all-gather | bytes 270336 | tf_op jit(solution)/shard_map/all_gather | solution.py:43
  57.9 58.8 %all-gather.2.cloned.1.call-done = f32[64,32768]{1,0:T(8,128)} async-done(((f32[64,1024]{1,0:T(8,128)}), f32[64,32768]{1,0:T(8,128)}) %all-gather.2.cloned.1.call-update) | async-done | bytes 8388624 | tf_op jit(solution)/shard_map/all_gather | solution.py:42
  116.6 157.3 %while.14 = (s32[]{:T(128)}, f32[64,1024]{1,0:T(8,128)S(1)}, f32[64,32768]{1,0:T(8,128)}, f32[2,32768]{1,0:T(2,128)S(1)}, f32[2,1024]{1,0:T(2,128)S(1)}, /*index...) while((s32[]{:T(128)}, f32[64,1024]{1,0:T(8,128)S(1)}, f32[64,32768]{1,0:T(8,128)}, ...), condition=%wide.region_1.0_spmd.clone, body=%wide.region_0.0_spmd.clone.sunk | while | flops 3250716672 | bytes 1695933 | solution.py:56
  116.7 0.1 constant_dynamic-slice_fusion.2
  116.8 19.5 %fusion.35 = f32[64,1024]{1,0:T(8,128)S(1)} fusion(f32[1024]{0:T(1024)S(1)} %bitcast.25, f32[4096]{0:T(1024)S(1)} %bitcast.23, f32[1024]{0:T(1024)S(1)} %bitcast.24, f32[4096]{0:T(1024)S(1)} %bitcast.22, f32[64,32768]{1,0:T(8,128)} %get-tuple-element.190, s32[]{:T(128)S(6)} %select_n.14, f32[64,1024]{1,0:T(8,128)S(1)} %get-tuple-element.179, ...), kind=kOutput, calls=%fused_computation.15.clone.1 | convolution fusion | flops 3250716672 | bytes 1613829 | tf_op jit(solution)/shard_map/while/body/eval_jaxpr/dot_general | solution.py:52
  136.3 0.1 constant_dynamic-slice_fusion.2
  136.4 19.5 %fusion.35 = f32[64,1024]{1,0:T(8,128)S(1)} fusion(f32[1024]{0:T(1024)S(1)} %bitcast.25, f32[4096]{0:T(1024)S(1)} %bitcast.23, f32[1024]{0:T(1024)S(1)} %bitcast.24, f32[4096]{0:T(1024)S(1)} %bitcast.22, f32[64,32768]{1,0:T(8,128)} %get-tuple-element.190, s32[]{:T(128)S(6)} %select_n.14, f32[64,1024]{1,0:T(8,128)S(1)} %get-tuple-element.179, ...), kind=kOutput, calls=%fused_computation.15.clone.1 | convolution fusion | flops 3250716672 | bytes 1613829 | tf_op jit(solution)/shard_map/while/body/eval_jaxpr/dot_general | solution.py:52
  155.9 0.1 constant_dynamic-slice_fusion.2
  156.1 19.5 %fusion.35 = f32[64,1024]{1,0:T(8,128)S(1)} fusion(f32[1024]{0:T(1024)S(1)} %bitcast.25, f32[4096]{0:T(1024)S(1)} %bitcast.23, f32[1024]{0:T(1024)S(1)} %bitcast.24, f32[4096]{0:T(1024)S(1)} %bitcast.22, f32[64,32768]{1,0:T(8,128)} %get-tuple-element.190, s32[]{:T(128)S(6)} %select_n.14, f32[64,1024]{1,0:T(8,128)S(1)} %get-tuple-element.179, ...), kind=kOutput, calls=%fused_computation.15.clone.1 | convolution fusion | flops 3250716672 | bytes 1613829 | tf_op jit(solution)/shard_map/while/body/eval_jaxpr/dot_general | solution.py:52
  175.6 0.1 constant_dynamic-slice_fusion.2
  175.7 19.5 %fusion.35 = f32[64,1024]{1,0:T(8,128)S(1)} fusion(f32[1024]{0:T(1024)S(1)} %bitcast.25, f32[4096]{0:T(1024)S(1)} %bitcast.23, f32[1024]{0:T(1024)S(1)} %bitcast.24, f32[4096]{0:T(1024)S(1)} %bitcast.22, f32[64,32768]{1,0:T(8,128)} %get-tuple-element.190, s32[]{:T(128)S(6)} %select_n.14, f32[64,1024]{1,0:T(8,128)S(1)} %get-tuple-element.179, ...), kind=kOutput, calls=%fused_computation.15.clone.1 | convolution fusion | flops 3250716672 | bytes 1613829 | tf_op jit(solution)/shard_map/while/body/eval_jaxpr/dot_general | solution.py:52
  195.2 0.1 constant_dynamic-slice_fusion.2
  195.4 19.5 %fusion.35 = f32[64,1024]{1,0:T(8,128)S(1)} fusion(f32[1024]{0:T(1024)S(1)} %bitcast.25, f32[4096]{0:T(1024)S(1)} %bitcast.23, f32[1024]{0:T(1024)S(1)} %bitcast.24, f32[4096]{0:T(1024)S(1)} %bitcast.22, f32[64,32768]{1,0:T(8,128)} %get-tuple-element.190, s32[]{:T(128)S(6)} %select_n.14, f32[64,1024]{1,0:T(8,128)S(1)} %get-tuple-element.179, ...), kind=kOutput, calls=%fused_computation.15.clone.1 | convolution fusion | flops 3250716672 | bytes 1613829 | tf_op jit(solution)/shard_map/while/body/eval_jaxpr/dot_general | solution.py:52
  214.9 0.1 constant_dynamic-slice_fusion.2
  215.0 19.5 %fusion.35 = f32[64,1024]{1,0:T(8,128)S(1)} fusion(f32[1024]{0:T(1024)S(1)} %bitcast.25, f32[4096]{0:T(1024)S(1)} %bitcast.23, f32[1024]{0:T(1024)S(1)} %bitcast.24, f32[4096]{0:T(1024)S(1)} %bitcast.22, f32[64,32768]{1,0:T(8,128)} %get-tuple-element.190, s32[]{:T(128)S(6)} %select_n.14, f32[64,1024]{1,0:T(8,128)S(1)} %get-tuple-element.179, ...), kind=kOutput, calls=%fused_computation.15.clone.1 | convolution fusion | flops 3250716672 | bytes 1613829 | tf_op jit(solution)/shard_map/while/body/eval_jaxpr/dot_general | solution.py:52
  234.5 0.1 constant_dynamic-slice_fusion.2
  234.6 19.5 %fusion.35 = f32[64,1024]{1,0:T(8,128)S(1)} fusion(f32[1024]{0:T(1024)S(1)} %bitcast.25, f32[4096]{0:T(1024)S(1)} %bitcast.23, f32[1024]{0:T(1024)S(1)} %bitcast.24, f32[4096]{0:T(1024)S(1)} %bitcast.22, f32[64,32768]{1,0:T(8,128)} %get-tuple-element.190, s32[]{:T(128)S(6)} %select_n.14, f32[64,1024]{1,0:T(8,128)S(1)} %get-tuple-element.179, ...), kind=kOutput, calls=%fused_computation.15.clone.1 | convolution fusion | flops 3250716672 | bytes 1613829 | tf_op jit(solution)/shard_map/while/body/eval_jaxpr/dot_general | solution.py:52
  254.2 0.1 constant_dynamic-slice_fusion.2
  254.3 19.5 %fusion.35 = f32[64,1024]{1,0:T(8,128)S(1)} fusion(f32[1024]{0:T(1024)S(1)} %bitcast.25, f32[4096]{0:T(1024)S(1)} %bitcast.23, f32[1024]{0:T(1024)S(1)} %bitcast.24, f32[4096]{0:T(1024)S(1)} %bitcast.22, f32[64,32768]{1,0:T(8,128)} %get-tuple-element.190, s32[]{:T(128)S(6)} %select_n.14, f32[64,1024]{1,0:T(8,128)S(1)} %get-tuple-element.179, ...), kind=kOutput, calls=%fused_computation.15.clone.1 | convolution fusion | flops 3250716672 | bytes 1613829 | tf_op jit(solution)/shard_map/while/body/eval_jaxpr/dot_general | solution.py:52
  274.0 0.1 stack_reshape.2
  274.1 2.1 stack.3
  276.2 4.0 %all-to-all-start = ((f32[8,32,2,1024]{3,2,1,0:T(2,128)}), f32[8,32,2,1024]{3,2,1,0:T(2,128)S(1)}, u32[]{:S(2)}, u32[]{:S(2)}) async-start(f32[8,32,2,1024]{3,2,1,0:T(2,128)} %stack.3), calls=%async_computation | async-start | bytes 4194304 | tf_op jit(solution)/shard_map/all_to_all | solution.py:13
  280.2 31.0 %all-to-all-done = f32[8,32,2,1024]{3,2,1,0:T(2,128)S(1)} async-done(((f32[8,32,2,1024]{3,2,1,0:T(2,128)}), f32[8,32,2,1024]{3,2,1,0:T(2,128)S(1)}, u32[]{:S(2)}, u32[]{:S(2)}) %all-to-all-start) | async-done | bytes 2097184 | tf_op jit(solution)/shard_map/all_to_all | solution.py:13
  311.2 2.6 copy.12
  313.8 2.7 reshape.58
  316.5 0.0 copy-done
  316.5 1.3 convolution_bitcast_fusion
  317.8 0.0 copy-start.1
  317.8 0.5 convolution_bitcast_fusion.1
  318.3 73.5 %psum.7 = f32[32,32]{1,0:T(8,128)} all-reduce(f32[32,32]{1,0:T(8,128)S(1)} %convolution_bitcast_fusion.1), channel_id=1, replica_groups=mesh['cell'=32,'period'=8] {'cell','period'}, use_global_device_ids=true, to_apply=%region_2.0 | all-reduce | flops 1024 | bytes 8192 | tf_op jit(solution)/shard_map/psum | solution.py:62
  391.8 0.0 copy-done.1
  (10 shorter events, 0.1 us)
Async XLA Ops:
  7.2 309.4 %copy-start = (f32[16,16]{1,0:T(8,128)S(1)}, f32[16,16]{1,0:T(8,128)}, u32[]{:S(2)}) copy-start(f32[16,16]{1,0:T(8,128)} %param.9) | copy-start | bytes 3076
  7.2 109.5 %all-gather.2.cloned.1.call-start = ((), (), s32[]{:S(2)}) async-start(), calls=%async_computation.1 | async-start | bytes 8650752 | tf_op jit(solution)/shard_map/all_gather | solution.py:42
  276.2 35.0 %all-to-all-start = ((f32[8,32,2,1024]{3,2,1,0:T(2,128)}), f32[8,32,2,1024]{3,2,1,0:T(2,128)S(1)}, u32[]{:S(2)}, u32[]{:S(2)}) async-start(f32[8,32,2,1024]{3,2,1,0:T(2,128)} %stack.3), calls=%async_computation | async-start | bytes 4194304 | tf_op jit(solution)/shard_map/all_to_all | solution.py:13
  317.8 74.0 %copy-start.1 = (f32[32,2,1024]{2,1,0:T(2,128)}, f32[32,2,1024]{2,1,0:T(2,128)S(1)}, u32[]{:S(2)}) copy-start(f32[32,2,1024]{2,1,0:T(2,128)S(1)} %convolution_bitcast_fusion) | copy-start | bytes 786436
Sparse Core Ops, SparseCore 0:
  11.4 105.2 all-gather.1
